TPU v7x, 32 devices: a whole 2x2x4 slice. The times are simulated.
32 devices in a mesh: tm: 2 (over x), band: 16 (over z, y, core).
Axes of the slice: x: 2, y: 2, z: 4, core: 2. Of those that a mesh axis runs over, the one named last changes fastest.
Arguments:
- samples: bfloat16 [512, 256, 2, 512], P('tm', 'band'), may hold values from -6 to 6
- weights: bfloat16 [256, 2, 512, 512], P('band', None, None, 'tm'), may hold values from -0.25 to 0.25
- prototype: float32 [1024], replicated, may hold values from 0.25 to 1
Outputs:
- beam_series: float32 [512, 131072], P('band', 'tm')
All inputs are finite; a program needn't handle non-finite values.
Results may differ from a plain program's by a relative error of at most 0.004.
Values may be sent and summed in bfloat16 or wider, within the bound.
A program may use at most 128 MiB of HBM per device.

v0:
```python
import math
import jax
import jax.numpy as jnp
from jax import lax
from jax.sharding import PartitionSpec as P

M = 512
K = 256
FIRST_BIN = 32


def passed_along(block, axis, distance):
    devices = range(lax.axis_size(axis))
    route = [(i - distance, i) for i in devices if i - distance in devices]
    return lax.ppermute(block, axis, route)


def synth_table(prototype):
    length = prototype.shape[0]
    bin_index = jnp.arange(K, dtype=jnp.int32) + FIRST_BIN
    tap_index = jnp.arange(length, dtype=jnp.int32)
    phase_index = bin_index[:, None] * tap_index[None, :] % M
    angles = phase_index.astype(jnp.float32) * (2.0 * math.pi / M)
    scaled = prototype[None, :] / math.sqrt(K)
    window_table = jnp.stack([jnp.cos(angles) * scaled, -jnp.sin(angles) * scaled], axis=1)
    return window_table.astype(jnp.bfloat16)


def intersection_add(frames, hop_size):
    pieces = frames.shape[-1] // hop_size
    pieces_view = frames.reshape(frames.shape[:-1] + (pieces, hop_size))
    leading = [(0, 0)] * (pieces_view.ndim - 3)
    intersection = jnp.zeros(
        pieces_view.shape[:-3] + (pieces_view.shape[-3] + pieces - 1, hop_size), frames.dtype
    )
    for lag in range(pieces):
        intersection = intersection + jnp.pad(
            pieces_view[..., lag, :], leading + [(lag, pieces - 1 - lag), (0, 0)]
        )
    return intersection


def beam_form(samples, weights):
    products = jnp.einsum("fkce,kdeb->bkdcf", samples, weights, preferred_element_type=jnp.float32)
    real_part = products[:, :, 0, 0] + products[:, :, 1, 1]
    imag_part = products[:, :, 0, 1] - products[:, :, 1, 0]
    return jnp.stack([real_part, imag_part], axis=2).astype(jnp.bfloat16)


def synthesize(spectra, window_table):
    return jnp.einsum("bkcf,kcn->bfn", spectra, window_table, preferred_element_type=jnp.float32)


def shards(samples, weights, prototype):
    hop_size = M // 2
    beam_parts = beam_form(samples, lax.all_gather(weights, "tm", axis=3, tiled=True))
    gathered = lax.all_to_all(beam_parts, "band", split_axis=0, concat_axis=1, tiled=True)
    window_table = synth_table(prototype)
    frame_total = gathered.shape[3]
    tail_rows = prototype.shape[0] // hop_size - 1
    frames = synthesize(gathered, window_table)
    summed = intersection_add(frames, hop_size)
    prev_tail = passed_along(summed[:, frame_total:], "tm", 1)
    block_out = summed[:, :frame_total]
    block_out = jnp.concatenate(
        [block_out[:, :tail_rows] + prev_tail, block_out[:, tail_rows:]], axis=1
    )
    return block_out.reshape(block_out.shape[0], frame_total * hop_size)


def solution(mesh):
    in_specs = (P("tm", "band", None, None), P("band", None, None, "tm"), P())
    out_specs = P("band", "tm")
    return jax.shard_map(shards, mesh=mesh, in_specs=in_specs, out_specs=out_specs, check_vma=False)
```

profile of v0, /device:TPU:16, one launch (start us, length us, event | category | flops | bytes accessed | tf_op | source)
XLA Modules:
  0.0 552.4 jit_solution(13992426558295163922)
XLA Ops:
  6.5 0.0 all-gather.2.cloned.1.call-start
  6.5 12.3 %copy.32 = bf16[16,2,512,256]{2,3,1,0:T(8,128)(2,1)} copy(bf16[16,2,512,256]{3,2,1,0:T(8,128)(2,1)} %param.4) | data formatting | bytes 16777216 | tf_op args[1]
  18.8 0.0 all-gather.2.cloned.1.call-update
  18.8 200.1 %all-gather.2.cloned.1.call-done = bf16[16,2,512,512]{2,3,1,0:T(8,128)(2,1)} async-done(((bf16[16,2,512,256]{2,3,1,0:T(8,128)(2,1)}), bf16[16,2,512,512]{2,3,1,0:T(8,128)(2,1)}) %all-gather.2.cloned.1.call-update) | async-done | bytes 16777232 | tf_op jit(solution)/shard_map/all_gather | solution.py:56
  218.9 27.4 %fusion.2 = f32[512,16,2,2,256]{4,0,3,2,1:T(8,128)} fusion(bf16[16,2,512,512]{2,3,1,0:T(8,128)(2,1)} %all-gather.2.cloned.1.call-done, bf16[256,16,2,512,1]{3,2,1,0,4:T(2,128)(2,1)} %bitcast.63), kind=kOutput, calls=%fused_computation.2 | convolution fusion | flops 8589934592 | bytes 58720256 | tf_op jit(solution)/shard_map/fkce,kdeb->bkdcf/dot_general | solution.py:44
  246.3 6.6 %fusion.10 = bf16[512,16,1,256]{3,0,1,2:T(8,128)(2,1)S(1)} fusion(f32[512,16,2,2,256]{4,0,3,2,1:T(8,128)} %fusion.2), kind=kLoop, calls=%fused_computation.21 | loop fusion | flops 4194304 | bytes 20971520 | tf_op jit(solution)/shard_map/sub | solution.py:46
  252.9 8.5 %fusion.9 = bf16[512,16,1,256]{3,0,1,2:T(8,128)(2,1)} fusion(f32[512,16,2,2,256]{4,0,3,2,1:T(8,128)} %fusion.2), kind=kLoop, calls=%fused_computation.20 | loop fusion | flops 4194304 | bytes 20971520 | tf_op jit(solution)/shard_map/add | solution.py:45
  261.4 6.3 %pad_maximum_fusion = bf16[512,16,2,256]{3,0,1,2:T(8,128)(2,1)} fusion(bf16[512,16,1,256]{3,0,1,2:T(8,128)(2,1)S(1)} %fusion.10, bf16[512,16,1,256]{3,0,1,2:T(8,128)(2,1)} %fusion.9), kind=kLoop, calls=%fused_computation.17 | loop fusion | flops 4194304 | bytes 16777216 | tf_op jit(solution)/shard_map/stack | solution.py:47
  267.8 11.4 %copy.36 = bf16[512,16,2,256]{3,1,2,0:T(8,128)(2,1)} copy(bf16[512,16,2,256]{3,0,1,2:T(8,128)(2,1)} %pad_maximum_fusion) | data formatting | bytes 16777216 | tf_op jit(solution)/shard_map/stack | solution.py:47
  279.2 0.0 copy-start.1
  279.2 6.2 %all-to-all-start = ((bf16[512,16,2,256]{3,1,2,0:T(8,128)(2,1)}), bf16[512,16,2,256]{3,1,2,0:T(8,128)(2,1)}, u32[]{:S(2)}, u32[]{:S(2)}) async-start(bf16[512,16,2,256]{3,1,2,0:T(8,128)(2,1)} %copy.36), calls=%async_computation | async-start | bytes 16777216 | tf_op jit(solution)/shard_map/all_to_all | solution.py:57
  285.4 0.0 copy-done.1
  285.4 4.6 multiply_convert_fusion.1
  290.0 0.1 pad_maximum_fusion.2
  290.1 177.8 %all-to-all-done = bf16[512,16,2,256]{3,1,2,0:T(8,128)(2,1)} async-done(((bf16[512,16,2,256]{3,1,2,0:T(8,128)(2,1)}), bf16[512,16,2,256]{3,1,2,0:T(8,128)(2,1)}, u32[]{:S(2)}, u32[]{:S(2)}) %all-to-all-start) | async-done | bytes 8388640 | tf_op jit(solution)/shard_map/all_to_all | solution.py:57
  467.9 8.0 %copy.37 = bf16[32,16,16,2,256]{4,2,1,3,0:T(8,128)(2,1)} copy(bf16[32,16,16,2,256]{4,2,3,0,1:T(8,128)(2,1)} %bitcast.7) | data formatting | bytes 16777216 | tf_op jit(solution)/shard_map/all_to_all | solution.py:57
  475.9 18.7 %convolution_bitcast_fusion = f32[32,256,4,256]{3,1,2,0:T(8,128)} fusion(bf16[32,256,2,256,1]{3,1,2,4,0:T(8,128)(2,1)} %bitcast.64, bf16[4,256,2,256]{3,1,0,2:T(8,128)(2,1)S(1)} %bitcast.65), kind=kOutput, calls=%fused_computation.3 | convolution fusion | flops 8589934592 | bytes 42991616 | tf_op jit(solution)/shard_map/bkcf,kcn->bfn/dot_general | solution.py:51
  494.6 20.8 %slice_bitcast_fusion.3 = (f32[32,256,256]{2,1,0:T(8,128)S(1)}, f32[32,256,256]{2,1,0:T(8,128)}, f32[32,256,256]{2,1,0:T(8,128)}, f32[32,256,256]{2,1,0:T(8,128)}) fusion(f32[32,256,4,256]{3,1,2,0:T(8,128)} %convolution_bitcast_fusion), kind=kLoop, calls=%fused_computation.10 | loop fusion | bytes 67108864 | tf_op jit(solution)/shard_map/squeeze | solution.py:38
  515.4 1.2 pad_add_fusion.3
  516.6 2.5 collective-permute-start
  519.1 13.6 %pad_add_fusion = f32[32,253,256]{2,1,0:T(8,128)} fusion(f32[32,256,256]{2,1,0:T(8,128)} %get-tuple-element.7, f32[32,256,256]{2,1,0:T(8,128)} %get-tuple-element.8, f32[32,256,256]{2,1,0:T(8,128)} %get-tuple-element.6, f32[32,256,256]{2,1,0:T(8,128)S(1)} %get-tuple-element.5), kind=kLoop, calls=%fused_computation.4 | loop fusion | flops 6217728 | bytes 41844736 | tf_op jit(solution)/shard_map/add | solution.py:37
  532.6 0.0 copy-start
  532.6 0.0 collective-permute-done
  532.6 1.3 add_add_fusion
  533.9 2.3 copy-done
  536.2 1.2 pad_maximum_fusion.1
  537.3 8.3 %copy.56 = f32[4,8,256,256]{3,1,2,0:T(8,128)} copy(f32[4,8,256,256]{3,2,1,0:T(8,128)S(1)} %bitcast.62) | data formatting | bytes 16777216
  (2 shorter events, 0.0 us)
Async XLA Ops:
  6.5 212.4 %all-gather.2.cloned.1.call-start = ((), (), s32[]{:S(2)}) async-start(), calls=%async_computation.1 | async-start | bytes 25165824 | tf_op jit(solution)/shard_map/all_gather | solution.py:56
  279.2 6.2 %copy-start.1 = (f32[1024]{0:T(1024)S(1)}, f32[1024]{0:T(1024)}, u32[]{:S(2)}) copy-start(f32[1024]{0:T(1024)} %param.5) | copy-start | bytes 12292
  279.2 188.7 %all-to-all-start = ((bf16[512,16,2,256]{3,1,2,0:T(8,128)(2,1)}), bf16[512,16,2,256]{3,1,2,0:T(8,128)(2,1)}, u32[]{:S(2)}, u32[]{:S(2)}) async-start(bf16[512,16,2,256]{3,1,2,0:T(8,128)(2,1)} %copy.36), calls=%async_computation | async-start | bytes 16777216 | tf_op jit(solution)/shard_map/all_to_all | solution.py:57
  516.6 16.0 %collective-permute-start = (f32[32,3,256]{2,1,0:T(4,128)S(1)}, f32[32,3,256]{2,1,0:T(4,128)S(1)}, u32[]{:S(2)}, u32[]{:S(2)}) collective-permute-start(f32[32,3,256]{2,1,0:T(4,128)S(1)} %pad_add_fusion.3), channel_id=1, source_target_pairs={{0,16},{1,17},{2,18},{3,19},{4,20},{5,21},{6,22},{7,23},{8,24},{9,... | collective-permute-start | bytes 294920 | tf_op jit(solution)/shard_map/ppermute | solution.py:15
  532.6 3.5 copy-start
Sparse Core Ops, SparseCore 0:
  19.0 199.8 all-gather.1
where the time goes:
time: 553 us; the launch traced here: 552 us
  waiting for transfers between devices  378 us (68%)
  local copies, waits for them, and re-layouts  63 us (11%)
  matrix products  46.1 us (8%)
  other arithmetic  43.4 us (8%)
  between operations  13.5 us (2%)
  starting transfers between devices  8.68 us (2%)
    all_gather x1, waiting for transfers between devices, shards(): lax.all_gather(weights, 'tm', axis=3, tiled=True)  200 us
    all_to_all x1, waiting for transfers between devices, shards(): lax.all_to_all(beam_parts, 'band', split_axis=0, concat_axis=1, tiled=True)  178 us
    dot_general x1, matrix products, beam_form(): jnp.einsum('fkce,kdeb->bkdcf', samples, weights, preferred_element_type=j...  27.4 us
    unnamed x6, local copies, waits for them, and re-layouts  22.8 us
    squeeze x1, local copies, waits for them, and re-layouts, intersection_add(): pieces_view[..., lag, :]  20.8 us
    dot_general x1, matrix products, synthesize(): jnp.einsum('bkcf,kcn->bfn', spectra, window_table, preferred_element_type...  18.7 us
    add x1, other arithmetic, intersection_add(): intersection + jnp.pad(pieces_view[..., lag, :], leading + [(lag, pieces...  13.6 us
    another operation x1, local copies, waits for them, and re-layouts, beam_form(): return jnp.stack([real_part, imag_part], axis=2).astype(jnp.bfloat16)  11.4 us
  transfers between devices with their start and end apart: 3, of which 2 were waited for; matrix products, arithmetic and copies ran while one was open for 3% of the time, Pallas kernels for 0%

commit v1 on v0

--- a/solution.py
+++ b/solution.py
@@ -54,7 +54,11 @@
 def shards(samples, weights, prototype):
     hop_size = M // 2
     beam_parts = beam_form(samples, lax.all_gather(weights, "tm", axis=3, tiled=True))
-    gathered = lax.all_to_all(beam_parts, "band", split_axis=0, concat_axis=1, tiled=True)
+    b_now = jax.lax.psum(1, "band")
+    after = jnp.split(beam_parts, b_now, 0)
+    frame_out = jnp.stack(after, 0)
+    newest = jax.lax.all_to_all(frame_out, "band", 0, 0)
+    gathered = jnp.concatenate(newest, axis=1)
     window_table = synth_table(prototype)
     frame_total = gathered.shape[3]
     tail_rows = prototype.shape[0] // hop_size - 1

time: 553 us -> 550 us (level)
  local copies, waits for them, and re-layouts: 63 us -> 55.1 us
    unnamed x0 -> x15, other arithmetic: none -> 12.4 us
    reshape x0 -> x1, local copies, waits for them, and re-layouts: none -> 11.5 us  [shards(): gathered = jnp.concatenate(newest, axis=1)]
    another operation x1 -> x0, local copies, waits for them, and re-layouts: 11.4 us -> none  [beam_form(): return jnp.stack([real_part, imag_part], axis=2).astype(jnp.bfloat16)]
    all_to_all x1 -> x0, local copies, waits for them, and re-layouts: 8.01 us -> none  [shards(): lax.all_to_all(beam_parts, 'band', split_axis=0, concat_axis=1, tiled=True)]
where the time goes in v1:
time: 550 us; the launch traced here: 549 us
  waiting for transfers between devices  378 us (69%)
  local copies, waits for them, and re-layouts  55.1 us (10%)
  other arithmetic  47.9 us (9%)
  matrix products  46.1 us (8%)
  between operations  13.5 us (2%)
  starting transfers between devices  8.68 us (2%)
    all_gather x1, waiting for transfers between devices, shards(): lax.all_gather(weights, 'tm', axis=3, tiled=True)  200 us
    all_to_all x1, waiting for transfers between devices, shards(): newest = jax.lax.all_to_all(frame_out, 'band', 0, 0)  178 us
    dot_general x1, matrix products, beam_form(): jnp.einsum('fkce,kdeb->bkdcf', samples, weights, preferred_element_type=j...  27.4 us
    unnamed x6, local copies, waits for them, and re-layouts  22.8 us
    squeeze x1, local copies, waits for them, and re-layouts, intersection_add(): pieces_view[..., lag, :]  20.8 us
    dot_general x1, matrix products, synthesize(): jnp.einsum('bkcf,kcn->bfn', spectra, window_table, preferred_element_type...  18.7 us
    add x1, other arithmetic, intersection_add(): intersection + jnp.pad(pieces_view[..., lag, :], leading + [(lag, pieces...  13.3 us
    unnamed x15, other arithmetic  12.4 us
  transfers between devices with their start and end apart: 3, of which 2 were waited for; matrix products, arithmetic and copies ran while one was open for 3% of the time, Pallas kernels for 0%

profile of v1, /device:TPU:16, one launch (start us, length us, event | category | flops | bytes accessed | tf_op | source)
XLA Modules:
  0.0 549.1 jit_solution(10817504798415944509)
XLA Ops:
  6.5 0.0 all-gather.2.cloned.1.call-start
  6.5 12.3 %copy.11 = bf16[16,2,512,256]{2,3,1,0:T(8,128)(2,1)} copy(bf16[16,2,512,256]{3,2,1,0:T(8,128)(2,1)} %param.4) | data formatting | bytes 16777216 | tf_op args[1]
  18.8 0.0 all-gather.2.cloned.1.call-update
  18.8 200.1 %all-gather.2.cloned.1.call-done = bf16[16,2,512,512]{2,3,1,0:T(8,128)(2,1)} async-done(((bf16[16,2,512,256]{2,3,1,0:T(8,128)(2,1)}), bf16[16,2,512,512]{2,3,1,0:T(8,128)(2,1)}) %all-gather.2.cloned.1.call-update) | async-done | bytes 16777232 | tf_op jit(solution)/shard_map/all_gather | solution.py:56
  218.9 27.4 %fusion.2 = f32[512,16,2,2,256]{4,0,3,2,1:T(8,128)} fusion(bf16[16,2,512,512]{2,3,1,0:T(8,128)(2,1)} %all-gather.2.cloned.1.call-done, bf16[256,16,2,512,1]{3,2,1,0,4:T(2,128)(2,1)} %bitcast.95), kind=kOutput, calls=%fused_computation.32 | convolution fusion | flops 8589934592 | bytes 58720256 | tf_op jit(solution)/shard_map/fkce,kdeb->bkdcf/dot_general | solution.py:44
  246.3 6.6 %fusion.10 = bf16[512,16,1,256]{3,0,1,2:T(8,128)(2,1)S(1)} fusion(f32[512,16,2,2,256]{4,0,3,2,1:T(8,128)} %fusion.2), kind=kLoop, calls=%fused_computation.50 | loop fusion | flops 4194304 | bytes 20971520 | tf_op jit(solution)/shard_map/sub | solution.py:46
  252.9 6.4 %fusion.9 = bf16[512,16,1,256]{3,0,1,2:T(8,128)(2,1)S(1)} fusion(f32[512,16,2,2,256]{4,0,3,2,1:T(8,128)} %fusion.2), kind=kLoop, calls=%fused_computation.49 | loop fusion | flops 4194304 | bytes 20971520 | tf_op jit(solution)/shard_map/add | solution.py:45
  259.3 0.8 bitcast_dynamic-update-slice_fusion.14
  260.1 0.8 bitcast_dynamic-update-slice_fusion.13
  261.0 0.8 bitcast_dynamic-update-slice_fusion.12
  261.8 0.8 bitcast_dynamic-update-slice_fusion.11
  262.6 0.8 bitcast_dynamic-update-slice_fusion.10
  263.4 0.8 bitcast_dynamic-update-slice_fusion.9
  264.3 0.8 bitcast_dynamic-update-slice_fusion.8
  265.1 0.8 bitcast_dynamic-update-slice_fusion.7
  265.9 0.8 bitcast_dynamic-update-slice_fusion.6
  266.8 0.8 bitcast_dynamic-update-slice_fusion.5
  267.6 0.8 bitcast_dynamic-update-slice_fusion.4
  268.4 0.8 bitcast_dynamic-update-slice_fusion.3
  269.2 0.8 bitcast_dynamic-update-slice_fusion.2
  270.1 0.8 bitcast_dynamic-update-slice_fusion.1
  270.9 0.8 bitcast_dynamic-update-slice_fusion
  271.7 0.8 fusion.35
  272.5 0.0 copy-start.1
  272.6 6.2 %all-to-all-start = ((bf16[16,32,16,2,256]{4,1,2,3,0:T(8,128)(2,1)}), bf16[16,32,16,2,256]{4,1,2,3,0:T(8,128)(2,1)}, u32[]{:S(2)}, u32[]{:S(2)}) async-start(bf16[16,32,16,2,256]{4,1,2,3,0:T(8,128)(2,1)} %fusion.35), calls=%async_computation | async-start | bytes 16777216 | tf_op jit(solution)/shard_map/all_to_all | solution.py:60
  278.8 0.0 copy-done.1
  278.8 4.6 multiply_convert_fusion.1
  283.4 0.1 pad_maximum_fusion.1
  283.5 177.8 %all-to-all-done = bf16[16,32,16,2,256]{4,1,2,3,0:T(8,128)(2,1)} async-done(((bf16[16,32,16,2,256]{4,1,2,3,0:T(8,128)(2,1)}), bf16[16,32,16,2,256]{4,1,2,3,0:T(8,128)(2,1)}, u32[]{:S(2)}, u32[]{:S(2)}) %all-to-all-start) | async-done | bytes 8388640 | tf_op jit(solution)/shard_map/all_to_all | solution.py:60
  461.3 11.5 %copy.15 = bf16[32,16,16,2,256]{4,2,1,3,0:T(8,128)(2,1)} copy(bf16[32,16,16,2,256]{4,0,2,3,1:T(8,128)(2,1)} %bitcast.22) | data formatting | bytes 16777216 | tf_op jit(solution)/shard_map/reshape | solution.py:61
  472.8 18.7 %convolution_bitcast_fusion = f32[32,256,4,256]{3,1,2,0:T(8,128)} fusion(bf16[32,256,2,256,1]{3,1,2,4,0:T(8,128)(2,1)} %bitcast.96, bf16[4,256,2,256]{3,1,0,2:T(8,128)(2,1)S(1)} %bitcast.97), kind=kOutput, calls=%fused_computation.33 | convolution fusion | flops 8589934592 | bytes 42991616 | tf_op jit(solution)/shard_map/bkcf,kcn->bfn/dot_general | solution.py:51
  491.5 20.8 %slice_bitcast_fusion.3 = (f32[32,256,256]{2,1,0:T(8,128)S(1)}, f32[32,256,256]{2,1,0:T(8,128)}, f32[32,256,256]{2,1,0:T(8,128)}, f32[32,256,256]{2,1,0:T(8,128)}) fusion(f32[32,256,4,256]{3,1,2,0:T(8,128)} %convolution_bitcast_fusion), kind=kLoop, calls=%fused_computation.40 | loop fusion | bytes 67108864 | tf_op jit(solution)/shard_map/squeeze | solution.py:38
  512.3 1.2 pad_add_fusion.3
  513.5 2.5 collective-permute-start
  516.0 13.3 %pad_add_fusion = f32[32,253,256]{2,1,0:T(8,128)} fusion(f32[32,256,256]{2,1,0:T(8,128)} %get-tuple-element.7, f32[32,256,256]{2,1,0:T(8,128)} %get-tuple-element.8, f32[32,256,256]{2,1,0:T(8,128)} %get-tuple-element.6, f32[32,256,256]{2,1,0:T(8,128)S(1)} %get-tuple-element.5), kind=kLoop, calls=%fused_computation.34 | loop fusion | flops 6217728 | bytes 41844736 | tf_op jit(solution)/shard_map/add | solution.py:37
  529.3 0.0 copy-start
  529.3 0.0 collective-permute-done
  529.3 1.3 add_add_fusion
  530.6 2.3 copy-done
  532.8 1.2 pad_maximum_fusion
  534.0 8.3 %copy.34 = f32[4,8,256,256]{3,1,2,0:T(8,128)} copy(f32[4,8,256,256]{3,2,1,0:T(8,128)S(1)} %bitcast.94) | data formatting | bytes 16777216
  (2 shorter events, 0.0 us)
Async XLA Ops:
  6.5 212.4 %all-gather.2.cloned.1.call-start = ((), (), s32[]{:S(2)}) async-start(), calls=%async_computation.1 | async-start | bytes 25165824 | tf_op jit(solution)/shard_map/all_gather | solution.py:56
  272.5 6.2 %copy-start.1 = (f32[1024]{0:T(1024)S(1)}, f32[1024]{0:T(1024)}, u32[]{:S(2)}) copy-start(f32[1024]{0:T(1024)} %param.5) | copy-start | bytes 12292
  272.6 188.7 %all-to-all-start = ((bf16[16,32,16,2,256]{4,1,2,3,0:T(8,128)(2,1)}), bf16[16,32,16,2,256]{4,1,2,3,0:T(8,128)(2,1)}, u32[]{:S(2)}, u32[]{:S(2)}) async-start(bf16[16,32,16,2,256]{4,1,2,3,0:T(8,128)(2,1)} %fusion.35), calls=%async_computation | async-start | bytes 16777216 | tf_op jit(solution)/shard_map/all_to_all | solution.py:60
  513.5 15.8 %collective-permute-start = (f32[32,3,256]{2,1,0:T(4,128)S(1)}, f32[32,3,256]{2,1,0:T(4,128)S(1)}, u32[]{:S(2)}, u32[]{:S(2)}) collective-permute-start(f32[32,3,256]{2,1,0:T(4,128)S(1)} %pad_add_fusion.3), channel_id=1, source_target_pairs={{0,16},{1,17},{2,18},{3,19},{4,20},{5,21},{6,22},{7,23},{8,24},{9,... | collective-permute-start | bytes 294920 | tf_op jit(solution)/shard_map/ppermute | solution.py:15
  529.3 3.5 copy-start
Sparse Core Ops, SparseCore 0:
  19.0 199.8 all-gather.1
